TPU v7x, 512 devices: a whole 4x8x8 slice. The times are simulated.
512 devices in a mesh: sta: 64 (over y, x, z_hi), win: 8 (over z_lo, core).
Axes of the slice: x: 4, y: 8, z: 8 (z_hi: 2, z_lo: 4; z = z_hi * 4 + z_lo), core: 2. Of those that a mesh axis runs over, the one named last changes fastest.
Arguments:
- spectra: float32 [16, 256, 2, 3, 1664], P('win', 'sta')
- flags: int32 [16, 256], P('win', 'sta'), may hold values 0 or 1
- owners: int32 [4], replicated, may hold values from 0 to 63, as said below
- source_slots: int32 [4, 4], replicated, may hold values from 0 to 3, as said below
Outputs:
- correlations: float32 [4, 4, 3, 256, 3, 768], P(None, None, None, 'sta')
Inputs may be any that keep to these rules, and one draw needn't show every extreme that they name: `owners`: the index of a block of 4 stations along sta. `source_slots`: distinct within a step.
All inputs are finite; a program needn't handle non-finite values. No bound on the sum of `flags` on one device may be relied on, other than what follows from the above.
Results may differ from a plain program's by a relative error of at most 0.0037.
Values sent between devices are 32-bit elements; how exact they have to be, the bound alone decides.
A program may use at most 64 MiB of HBM per device.

v0:
```python
import math
import jax
import jax.numpy as jnp
from jax import lax
from jax.sharding import PartitionSpec as P

NLAG = 768
STEPS = 4


def spread(value, axis, source):
    kept = jnp.where(lax.axis_index(axis) == source, value, 0).astype(value.dtype)
    return lax.psum(kept, axis)


def whiten(spectra):
    shape = spectra.shape
    blocks = spectra.reshape(shape[0], shape[1], 2, 3, shape[4] // 64, 64)
    power = jnp.mean(blocks * blocks, axis=(2, 3, 5), keepdims=True)
    return (blocks / jnp.sqrt(power + 1e-06)).reshape(shape)


def lag_table(bins, lags, windows):
    freq = jnp.arange(bins, dtype=jnp.int32) + 360
    shift = jnp.arange(lags, dtype=jnp.int32) - lags // 2
    phase = jnp.mod(freq[:, None] * shift[None, :], 7200).astype(jnp.float32) * (
        2.0 * math.pi / 7200.0
    )
    scale = 1.0 / math.sqrt(windows * bins)
    return jnp.concatenate([jnp.cos(phase) * scale, -jnp.sin(phase) * scale], axis=0).astype(
        jnp.bfloat16
    )


def correlate(picked, receivers, table):
    src_re = picked[:, :, 0][:, :, :, None, None, :]
    src_im = picked[:, :, 1][:, :, :, None, None, :]
    rec_re = receivers[:, :, 0][:, None, None, :, :, :]
    rec_im = receivers[:, :, 1][:, None, None, :, :, :]
    real = jnp.sum(src_re * rec_re + src_im * rec_im, axis=0)
    imag = jnp.sum(src_im * rec_re - src_re * rec_im, axis=0)
    shape = real.shape
    bins = shape[4]
    rows = jnp.concatenate([real.reshape(-1, bins), imag.reshape(-1, bins)], axis=1).astype(
        jnp.bfloat16
    )
    lagged = jnp.dot(rows, table, preferred_element_type=jnp.float32)
    return lagged.reshape(shape[0], shape[1], shape[2], shape[3], table.shape[1])


def on_device(spectra, flags, owners, source_slots):
    win_count = spectra.shape[0]
    bins = spectra.shape[4]
    weighted = whiten(spectra) * flags.astype(jnp.float32)[:, :, None, None, None]
    table = lag_table(bins, NLAG, win_count * lax.axis_size("win"))
    outputs = []
    for step in range(STEPS):
        chosen = jnp.take(weighted, source_slots[step], axis=1)
        picked = spread(chosen, "sta", owners[step])
        partial_stack = correlate(picked, weighted, table)
        partial_stack = lax.psum(partial_stack, "win")
        outputs.append(partial_stack)
    stacked = jnp.stack(outputs)
    return stacked


def solution(mesh):
    return jax.shard_map(
        on_device,
        mesh=mesh,
        in_specs=(P("win", "sta", None, None, None), P("win", "sta"), P(), P()),
        out_specs=P(None, None, None, "sta", None, None),
        check_vma=False,
    )
```

profile of v0, /device:TPU:2, one launch (start us, length us, event | category | flops | bytes accessed | tf_op | source)
XLA Modules:
  0.0 1011.2 jit_solution(12105499621488720330)
XLA Ops:
  6.5 0.0 all-reduce.5.cloned.1.call-start
  6.5 0.7 convert_element_type.18
  7.2 1.5 fusion.30
  11.2 0.8 compare_and_fusion
  12.1 1.2 multiply_reduce_fusion
  13.3 0.1 reduce_sum.89
  13.4 0.1 reduce_sum.90
  13.6 0.1 div.21
  13.7 0.1 div.22
  13.8 1.1 divide_multiply_fusion
  14.9 0.9 gather_fusion.2
  15.9 0.9 gather_fusion.1
  16.8 0.9 gather_fusion.3
  17.7 0.9 gather_fusion
  18.6 1.2 bitcast_select_fusion
  19.8 1.2 bitcast_select_fusion.2
  21.1 0.0 all-reduce.5.cloned.1.call-update
  21.1 0.0 all-reduce.7.cloned.1.call-start
  21.2 0.2 fusion.29
  21.4 0.1 copy_bitcast_fusion.8
  21.5 23.4 %multiply_convert_fusion.1 = (bf16[1664,768]{1,0:T(8,128)(2,1)S(1)}, bf16[1664,768]{1,0:T(8,128)(2,1)}) fusion(s32[768]{0:T(1024)S(1)} %iota_add_fusion.1, s32[1664]{0:T(1024)S(1)} %iota_add_fusion), kind=kLoop, calls=%fused_computation.9 | loop fusion | flops 17891328 | bytes 5121536 | tf_op jit(solution)/shard_map/convert.12
  45.0 813.5 %all-reduce.5.cloned.1.call-done = (f32[2,4,2,3,1664]{4,2,3,0,1:T(2,128)}, f32[2,4,2,3,1664]{4,2,3,0,1:T(2,128)}, f32[2,4,2,3,1664]{4,2,3,0,1:T(2,128)}, f32[2,4,2,3,1664]{4,2,3,0,1:T(2,128)}) async-done(((f32[2,4,2,3,1664]{4,2,3,0,1:T(2,128)}, f32[2,4,2,3,1664]{4,2,3,0,1:T(2,128)}, f32[2,4,2,3,1664]{4,2,3,0,1:T(2,128)}, f32[2,4,2,3,1664]{4,2,3,0,1:T(2,128)}), (f32[2,4,2,3,1664]{4,2,3,0,1:T(2,128)}, ...) | async-done | bytes 1277968 | tf_op jit(solution)/shard_map/psum | solution.py:13
  858.4 1.4 fusion.28
  859.8 0.1 copy.90
  859.9 0.1 copy.89
  860.0 1.3 fusion.27
  861.3 0.1 copy.87
  861.4 0.1 copy.88
  861.4 0.0 copy-done.5
  861.5 0.2 fusion.26
  861.7 0.1 copy.85
  861.8 0.1 copy.86
  861.8 0.2 fusion.25
  862.1 0.1 copy.83
  862.2 0.1 copy.84
  862.2 14.1 %add_reduce_fusion.3 = (bf16[4,3,4,3,1664]{4,2,3,1,0:T(4,128)(2,1)S(1)}, bf16[4,3,4,3,1664]{4,2,3,1,0:T(4,128)(2,1)}, bf16[4,3,4,3,1664]{4,2,3,1,0:T(4,128)(2,1)...) fusion(f32[2,4,3,1664]{3,1,2,0:T(4,128)S(1)} %get-tuple-element, ...), kind=kLoop, calls=%fused_computation.22 | loop fusion | flops 13418496 | bytes 5431296 | tf_op jit(solution)/shard_map/reduce_sum | solution.py:40
  876.4 0.2 copy.44
  876.6 1.2 reshape.80
  877.8 1.3 copy.45
  879.1 1.2 reshape.81
  880.2 1.3 copy.51
  881.5 1.2 reshape.84
  882.7 1.3 copy.50
  884.0 1.2 reshape.83
  885.1 1.3 copy.57
  886.4 1.2 reshape.87
  887.6 1.3 copy.56
  888.9 1.2 reshape.86
  890.1 1.3 copy.63
  891.3 1.2 reshape.90
  892.5 1.3 copy.62
  893.8 1.2 reshape.89
  895.0 3.8 fusion.5
  898.8 2.0 stack.15
  900.8 3.4 fusion.17
  904.2 2.0 stack.18
  906.2 3.8 fusion.13
  910.0 2.0 stack.17
  912.0 3.4 fusion.9
  915.5 2.0 stack.16
  917.5 0.0 all-reduce.7.cloned.1.call-update
  917.5 83.0 %all-reduce.7.cloned.1.call-done = (f32[1,4,3,4,3,768]{5,4,3,2,1,0:T(4,128)}, f32[1,4,3,4,3,768]{5,4,3,2,1,0:T(4,128)}, f32[1,4,3,4,3,768]{5,4,3,2,1,0:T(4,128)}, f32[1,4,3,4,3,768]{5,4,3,2,1,0:T(4,128)}) async-done(((f32[1,4,3,4,3,768]{5,4,3,2,1,0:T(4,128)}, f32[1,4,3,4,3,768]{5,4,3,2,1,0:T(4,128)}, f32[1,4,3,4,3,768]{5,4,3,2,1,0:T(4,128)}, f32[1,4,3,4,3,768]{5,4,3,2,1,0:T(4,128)}), ...) | async-done | bytes 1769488 | tf_op jit(solution)/shard_map/psum | solution.py:61
  1000.5 2.2 pad_maximum_fusion.1
  1002.7 1.7 copy.64
  (18 shorter events, 0.1 us)
Async XLA Ops:
  6.5 851.9 %all-reduce.5.cloned.1.call-start = ((), (), s32[]{:S(2)}) async-start(), calls=%async_computation | async-start | bytes 2555904 | tf_op jit(solution)/shard_map/psum | solution.py:13
  21.1 979.4 %all-reduce.7.cloned.1.call-start = ((), (), s32[]{:S(2)}) async-start(), calls=%async_computation.1 | async-start | bytes 4718592 | tf_op jit(solution)/shard_map/psum | solution.py:61
  858.4 3.0 copy-start.5
  858.4 3.4 copy-start.4
  895.0 5.8 copy-start.2
  895.0 5.8 copy-start.3
  906.2 5.8 copy-start
  906.2 5.8 copy-start.1
Sparse Core Ops, SparseCore 0:
  21.2 837.1 all-reduce.4
  917.6 82.8 all-reduce.6
where the time goes:
time: 1010 us
  waiting for transfers between devices  896 us (89%)
  other arithmetic  46.3 us (5%)
  local copies, waits for them, and re-layouts  37.7 us (4%)
  between operations  16.2 us (2%)
  matrix products  14.4 us (1%)
    psum x1, waiting for transfers between devices, spread(): return lax.psum(kept, axis)  813 us
    psum x1, waiting for transfers between devices, on_device(): partial_stack = lax.psum(partial_stack, 'win')  83 us
    another operation x1, other arithmetic  23.4 us
  transfers between devices with their start and end apart: 2, of which 2 were waited for; matrix products, arithmetic and copies ran while one was open for 2% of the time, Pallas kernels for 0%

commit v1 on v0

--- a/solution.py
+++ b/solution.py
@@ -58,7 +58,7 @@
         chosen = jnp.take(weighted, source_slots[step], axis=1)
         picked = spread(chosen, "sta", owners[step])
         partial_stack = correlate(picked, weighted, table)
-        partial_stack = lax.psum(partial_stack, "win")
+        partial_stack = jnp.sum(lax.all_gather(partial_stack, "win"), axis=0)
         outputs.append(partial_stack)
     stacked = jnp.stack(outputs)
     return stacked

time: 1010 us -> 1100 us (1.089)
  waiting for transfers between devices: 896 us -> 976 us
    all_gather x0 -> x4, waiting for transfers between devices: none -> 163 us  [on_device(): partial_stack = jnp.sum(lax.all_gather(partial_stack, 'win'), axis=0)]
    psum x1 -> x0, waiting for transfers between devices: 83 us -> none  [on_device(): partial_stack = lax.psum(partial_stack, 'win')]
  transfers between devices with their start and end apart: 2 -> 5, of which waited for: 2 -> 5; matrix products, arithmetic and copies ran while one was open for 2% -> 6% of each run, Pallas kernels for 0% -> 0%
where the time goes in v1:
time: 1100 us
  waiting for transfers between devices  976 us (89%)
  other arithmetic  55.2 us (5%)
  local copies, waits for them, and re-layouts  38.8 us (4%)
  between operations  16 us (1%)
  matrix products  14.9 us (1%)
    psum x1, waiting for transfers between devices, spread(): return lax.psum(kept, axis)  813 us
    all_gather x4, waiting for transfers between devices, on_device(): partial_stack = jnp.sum(lax.all_gather(partial_stack, 'win'), axis=0)  163 us
    another operation x1, other arithmetic  23.5 us
  transfers between devices with their start and end apart: 5, of which 5 were waited for; matrix products, arithmetic and copies ran while one was open for 6% of the time, Pallas kernels for 0%

profile of v1, /device:TPU:2, one launch (start us, length us, event | category | flops | bytes accessed | tf_op | source)
XLA Modules:
  0.0 1101.4 jit_solution(11347958544234967714)
XLA Ops:
  6.5 0.7 convert_element_type.18
  7.2 1.5 fusion.30
  11.2 0.8 compare_and_fusion
  12.1 1.2 multiply_reduce_fusion
  13.3 0.1 reduce_sum.125
  13.8 1.1 divide_multiply_fusion
  14.9 0.9 gather_fusion.2
  15.9 0.9 gather_fusion.1
  16.8 0.9 gather_fusion.3
  17.7 0.9 gather_fusion
  18.6 1.2 bitcast_select_fusion
  19.8 1.2 bitcast_select_fusion.2
  21.1 0.2 all-gather.5.cloned.1.call-start
  21.3 0.2 fusion.29
  21.7 23.5 %multiply_convert_fusion.1 = (bf16[1664,768]{1,0:T(8,128)(2,1)S(1)}, bf16[1664,768]{1,0:T(8,128)(2,1)}) fusion(s32[768]{0:T(1024)S(1)} %iota_add_fusion.1, s32[1664]{0:T(1024)S(1)} %iota_add_fusion), kind=kLoop, calls=%fused_computation.9 | loop fusion | flops 17891328 | bytes 5121536 | tf_op jit(solution)/shard_map/convert.12
  45.2 812.8 %all-reduce.3.cloned.1.call-done = (f32[2,4,2,3,1664]{4,2,3,0,1:T(2,128)}, f32[2,4,2,3,1664]{4,2,3,0,1:T(2,128)}, f32[2,4,2,3,1664]{4,2,3,0,1:T(2,128)}, f32[2,4,2,3,1664]{4,2,3,0,1:T(2,128)}) async-done(((f32[2,4,2,3,1664]{4,2,3,0,1:T(2,128)}, f32[2,4,2,3,1664]{4,2,3,0,1:T(2,128)}, f32[2,4,2,3,1664]{4,2,3,0,1:T(2,128)}, f32[2,4,2,3,1664]{4,2,3,0,1:T(2,128)}), (f32[2,4,2,3,1664]{4,2,3,0,1:T(2,128)}, ...) | async-done | bytes 1277968 | tf_op jit(solution)/shard_map/psum | solution.py:13
  857.9 1.4 fusion.28
  859.5 1.3 fusion.27
  860.9 0.2 fusion.26
  861.3 0.2 fusion.25
  861.7 13.9 %add_reduce_fusion.3 = (bf16[4,3,4,3,1664]{4,2,3,1,0:T(4,128)(2,1)S(1)}, bf16[4,3,4,3,1664]{4,2,3,1,0:T(4,128)(2,1)}, bf16[4,3,4,3,1664]{4,2,3,1,0:T(4,128)(2,1)...) fusion(f32[2,4,3,1664]{3,1,2,0:T(4,128)S(1)} %get-tuple-element, ...), kind=kLoop, calls=%fused_computation.22 | loop fusion | flops 13418496 | bytes 5431296 | tf_op jit(solution)/shard_map/reduce_sum | solution.py:40
  875.7 0.2 copy.68
  875.9 1.2 reshape.68
  877.1 1.3 copy.69
  878.4 1.2 reshape.69
  879.6 3.7 fusion.5
  883.3 1.2 all_gather_reshape.12
  884.5 0.9 copy.70
  885.4 0.3 all-gather.11.cloned.1.call-start
  885.7 1.3 copy.93
  886.9 1.2 reshape.75
  888.1 1.3 copy.92
  889.4 1.2 reshape.74
  890.6 3.8 fusion.17
  894.4 1.2 all_gather_reshape.15
  895.6 0.9 copy.94
  896.6 1.3 copy.85
  897.9 1.2 reshape.73
  899.0 1.3 copy.84
  900.3 1.2 reshape.72
  901.5 3.7 fusion.13
  905.2 1.2 all_gather_reshape.14
  906.4 0.9 copy.86
  907.4 1.3 copy.77
  908.7 1.2 reshape.71
  909.9 1.3 copy.76
  911.1 1.2 reshape.70
  912.4 3.7 fusion.9
  916.1 1.2 all_gather_reshape.13
  917.3 0.9 copy.78
  918.2 14.1 %all-gather.5.cloned.1.call-done = f32[8,4,3,4,3,768]{5,3,4,2,1,0:T(4,128)} async-done(((f32[1,4,3,4,3,768]{5,3,4,2,1,0:T(4,128)}), f32[8,4,3,4,3,768]{5,3,4,2,1,0:T(4,128)}) %all-gather.5.cloned.1.call-update) | async-done | bytes 3538960 | tf_op jit(solution)/shard_map/all_gather | solution.py:61
  932.3 2.7 reduce_sum.129
  934.9 0.2 copy.126
  935.1 49.7 %all-gather.11.cloned.1.call-done = f32[8,4,3,4,3,768]{5,3,4,2,1,0:T(4,128)} async-done(((f32[1,4,3,4,3,768]{5,3,4,2,1,0:T(4,128)}), f32[8,4,3,4,3,768]{5,3,4,2,1,0:T(4,128)}) %all-gather.11.cloned.1.call-update) | async-done | bytes 3538960 | tf_op jit(solution)/shard_map/all_gather | solution.py:61
  984.8 2.7 reduce_sum.138
  987.5 0.2 copy.123
  987.7 49.6 %all-gather.9.cloned.1.call-done = f32[8,4,3,4,3,768]{5,3,4,2,1,0:T(4,128)} async-done(((f32[1,4,3,4,3,768]{5,3,4,2,1,0:T(4,128)}), f32[8,4,3,4,3,768]{5,3,4,2,1,0:T(4,128)}) %all-gather.9.cloned.1.call-update) | async-done | bytes 3538960 | tf_op jit(solution)/shard_map/all_gather | solution.py:61
  1037.3 2.7 reduce_sum.135
  1039.9 0.2 copy.124
  1040.1 49.6 %all-gather.7.cloned.1.call-done = f32[8,4,3,4,3,768]{5,3,4,2,1,0:T(4,128)} async-done(((f32[1,4,3,4,3,768]{5,3,4,2,1,0:T(4,128)}), f32[8,4,3,4,3,768]{5,3,4,2,1,0:T(4,128)}) %all-gather.7.cloned.1.call-update) | async-done | bytes 3538960 | tf_op jit(solution)/shard_map/all_gather | solution.py:61
  1089.7 2.7 reduce_sum.132
  1092.4 0.2 copy.125
  1092.5 0.7 pad_maximum_fusion.1
  1093.2 1.7 copy.96
  (31 shorter events, 1.1 us)
Async XLA Ops:
  6.5 851.4 %all-reduce.3.cloned.1.call-start = ((), (), s32[]{:S(2)}) async-start(), calls=%async_computation.4 | async-start | bytes 2555904 | tf_op jit(solution)/shard_map/psum | solution.py:13
  21.1 911.2 %all-gather.5.cloned.1.call-start = ((), (), s32[]{:S(2)}) async-start(), calls=%async_computation | async-start | bytes 3981312 | tf_op jit(solution)/shard_map/all_gather | solution.py:61
  857.9 3.0 copy-start.1
  857.9 3.4 copy-start
  885.4 99.5 %all-gather.11.cloned.1.call-start = ((), (), s32[]{:S(2)}) async-start(), calls=%async_computation.3 | async-start | bytes 3981312 | tf_op jit(solution)/shard_map/all_gather | solution.py:61
  896.5 140.7 %all-gather.9.cloned.1.call-start = ((), (), s32[]{:S(2)}) async-start(), calls=%async_computation.2 | async-start | bytes 3981312 | tf_op jit(solution)/shard_map/all_gather | solution.py:61
  907.3 182.3 %all-gather.7.cloned.1.call-start = ((), (), s32[]{:S(2)}) async-start(), calls=%async_computation.1 | async-start | bytes 3981312 | tf_op jit(solution)/shard_map/all_gather | solution.py:61
Sparse Core Ops, SparseCore 0:
  21.2 836.6 all-reduce.2
  885.5 46.7 all-gather.4
  934.6 50.2 all-gather.10
  987.0 50.2 all-gather.8
  1039.4 50.2 all-gather.6
